TPU v7x, 32 devices: a whole 2x2x4 slice. The times are simulated.
32 devices in a mesh: groups: 2 (over y), panels: 4 (over z), cols: 2 (over x), phase: 2 (over core).
Axes of the slice: x: 2, y: 2, z: 4, core: 2. Of those that a mesh axis runs over, the one named last changes fastest.
Arguments:
- base_points: float32 [3, 512], P(None, ('groups', 'panels', 'cols')), parts along dimension 1, may hold values from -6 to 6
- control_points: float32 [3, 2048], replicated, may hold values from -6 to 6
- morph_weights: float32 [4, 3, 2048], P('groups'), parts along dimension 0, may hold values from -0.15 to 0.15
- connectivity: int32 [3, 1024], P(None, ('groups', 'panels', 'cols')), parts along dimension 1, may hold values from 0 to 255, as said below
- free_flags: int32 [1024], P(('groups', 'panels', 'cols')), parts along dimension 0, may hold values 0 or 1
- station_owner: int32 [1024, 1], P(('groups', 'panels', 'cols')), parts along dimension 0, may hold values from 0 to 7; in each aligned block of 64 rows (0 to 63, 64 to 127, ...) at most 20 rows name the same one
- variant_order: int32 [4], P('groups'), parts along dimension 0, may hold values from 0 to 1, each once
- load_velocity: float32 [64, 3], replicated, may hold values from -5 to 5
Outputs:
- shear: float32 [4, 64, 1024], P(('groups', 'phase'), None, ('panels', 'cols')), parts along dimension 0
- moment: float32 [4, 64, 1024], P(('groups', 'phase'), None, ('panels', 'cols')), parts along dimension 0
There are 2 independent parts, one for each index of `groups`. A program takes and returns all parts, laid end to end along the dimension named above; an argument that names none is the same for every part. Nothing has to cross between parts.
Inputs may be any that keep to these rules, and one draw needn't show every extreme that they name: `connectivity`: the vertices of panel i lie in block i // 64 of 32 consecutive vertices: from (i // 64) * 32 to (i // 64 + 1) * 32 - 1. `station_owner`: among the panels of one device (aligned blocks of 64 panels) no station owner is named more than 20 times. `variant_order`: each variant appears once.
All inputs are finite; a program needn't handle non-finite values. No bound on the sum of `free_flags` on one device may be relied on, other than what follows from the above.
Results may differ from a plain program's by a relative error of at most 0.0015.
Values may be sent and summed in bfloat16 or wider, within the bound.
A program may use at most 64 MiB of HBM per device.

v0:
```python
import math
import jax
import jax.numpy as jnp
from jax import lax
from jax.sharding import PartitionSpec as P

STATIONS = 128
HIGH = lax.Precision.HIGHEST
CORE_SQUARE = 0.0025
SKIN_SQUARE = 0.01


def prefix(shard, axis, combine, identity):
    length, index = (lax.axis_size(axis), lax.axis_index(axis))
    everything = jax.tree.map(lambda part: lax.all_gather(part, axis), shard)
    start = jax.tree.map(
        lambda part, zero: jnp.broadcast_to(jnp.asarray(zero, part.dtype), part.shape),
        shard,
        identity,
    )

    def step(k, before):
        reached = k < index
        new = combine(before, jax.tree.map(lambda part: part[k], everything))
        return jax.tree.map(lambda a, b: jnp.where(reached, a, b), new, before)

    return lax.fori_loop(0, length, step, start)


def panel_shape(moved_points, corner_rows):
    first_corner = jnp.take(moved_points, corner_rows[0], axis=2)
    second_corner = jnp.take(moved_points, corner_rows[1], axis=2)
    third_corner = jnp.take(moved_points, corner_rows[2], axis=2)
    centroid = (first_corner + second_corner + third_corner) / 3.0
    edge_one = second_corner - first_corner
    edge_two = third_corner - first_corner
    cross_x = edge_one[:, 1] * edge_two[:, 2] - edge_one[:, 2] * edge_two[:, 1]
    cross_y = edge_one[:, 2] * edge_two[:, 0] - edge_one[:, 0] * edge_two[:, 2]
    cross_z = edge_one[:, 0] * edge_two[:, 1] - edge_one[:, 1] * edge_two[:, 0]
    area = 0.5 * jnp.stack([cross_x, cross_y, cross_z], axis=1)
    weight = jnp.sqrt(jnp.sum(area * area, axis=1) + SKIN_SQUARE)
    return (centroid, area, weight)


def tile_block(targets, sources, strengths, kernel_scale):
    distance = (
        (targets[:, 0, :, None] - sources[:, 0, None, :]) ** 2
        + (targets[:, 1, :, None] - sources[:, 1, None, :]) ** 2
        + (targets[:, 2, :, None] - sources[:, 2, None, :]) ** 2
    )
    influence = (sources[:, 3, None, :] * kernel_scale * lax.rsqrt(distance + CORE_SQUARE)).astype(
        jnp.bfloat16
    )
    return jnp.einsum("mrn,mkn->mkr", influence, strengths, preferred_element_type=jnp.float32)


def tile_product(carry_sum, targets, sources, strengths, kernel_scale):
    columns = strengths.shape[2]
    block_width = columns
    for candidate in (2048, 1024, 512):
        if columns > candidate and columns % candidate == 0:
            block_width = candidate
            break
    if block_width == columns:
        return carry_sum + tile_block(targets, sources, strengths, kernel_scale)

    def block_step(step_index, running_sum):
        column_start = step_index * block_width
        part_sources = lax.dynamic_slice_in_dim(sources, column_start, block_width, 2)
        part_strengths = lax.dynamic_slice_in_dim(strengths, column_start, block_width, 2)
        return running_sum + tile_block(targets, part_sources, part_strengths, kernel_scale)

    return lax.fori_loop(0, columns // block_width, block_step, carry_sum)


def add_pairs(earlier, later):
    return (earlier[0] + later[0], earlier[1] + later[1])


def shards(
    base_points,
    control_points,
    morph_weights,
    connectivity,
    free_flags,
    station_owner,
    variant_order,
    load_velocity,
):
    owners = lax.axis_size(("panels", "cols"))
    owner_index = lax.axis_index(("panels", "cols"))
    phase_index = lax.axis_index("phase")
    variant_dev = variant_order.shape[0] // lax.axis_size("phase")
    vert_dev = base_points.shape[1]
    pan_dev = connectivity.shape[1]
    load_count = load_velocity.shape[0]
    panels_total = pan_dev * owners
    own_variants = lax.dynamic_slice_in_dim(
        variant_order, phase_index * variant_dev, variant_dev, 0
    )
    picker = (
        own_variants[:, None] == jnp.arange(variant_order.shape[0], dtype=jnp.int32)[None, :]
    ).astype(jnp.float32)
    chosen = jnp.einsum("mv,vac->mac", picker, morph_weights, precision=HIGH)
    distance = (
        (control_points[0][:, None] - base_points[0][None, :]) ** 2
        + (control_points[1][:, None] - base_points[1][None, :]) ** 2
        + (control_points[2][:, None] - base_points[2][None, :]) ** 2
    )
    basis_values = lax.rsqrt(1.0 + distance)
    moved_points = base_points[None] + jnp.einsum(
        "mac,cn->man", chosen, basis_values, precision=HIGH
    )
    local_corners = connectivity - owner_index * vert_dev
    centroid, area, weight = panel_shape(moved_points, local_corners)
    hull_mask = (1 - free_flags).astype(jnp.float32)
    boundary = (
        jnp.einsum("ka,man->mkn", load_velocity, area, precision=HIGH) * hull_mask[None, None, :]
    )
    first_strengths = boundary.astype(jnp.bfloat16)
    kernel_scale = 1.0 / (4.0 * math.pi * math.sqrt(panels_total))
    own_geometry = jnp.concatenate([centroid, weight[:, None, :]], axis=1)
    sources = lax.all_gather(own_geometry, "panels", axis=2, tiled=True)
    row_targets = lax.all_gather(centroid, "cols", axis=2, tiled=True)

    def apply_influence(strengths):
        empty_sum = jnp.zeros((variant_dev, load_count, row_targets.shape[2]), jnp.float32)
        partial_sums = tile_product(
            empty_sum,
            row_targets,
            sources,
            lax.all_gather(strengths, "panels", axis=2, tiled=True),
            kernel_scale,
        )
        return lax.psum_scatter(partial_sums, "cols", scatter_dimension=2, tiled=True)

    induced = apply_influence(first_strengths)
    second_strengths = (first_strengths.astype(jnp.float32) + (boundary - induced)).astype(
        jnp.bfloat16
    )
    pressure = apply_influence(second_strengths)
    panel_force = pressure * (area[:, 2, :] * hull_mask[None, :])[:, None, :]
    force_rows = panel_force.reshape(-1, pan_dev)
    capacity = max(2, 5 * pan_dev // (2 * owners))
    target_owner = station_owner[:, 0]
    panel_order = jnp.arange(pan_dev, dtype=jnp.int32)
    ahead = (target_owner[:, None] == target_owner[None, :]) & (
        panel_order[None, :] < panel_order[:, None]
    )
    slot_rank = jnp.sum(ahead.astype(jnp.int32), axis=1)
    slot_index = target_owner * capacity + slot_rank
    all_slots = jnp.arange(owners * capacity, dtype=jnp.int32)
    placed = slot_index[:, None] == all_slots[None, :]
    send_values = jnp.dot(force_rows, placed.astype(jnp.float32), precision=HIGH)
    station_bins = (owner_index * pan_dev + panel_order) % STATIONS
    send_bins = jnp.max(jnp.where(placed, station_bins[:, None], -1), axis=0)[None, :]
    recv_values, recv_bins = (
        lax.all_to_all(send_values, ("panels", "cols"), split_axis=1, concat_axis=1, tiled=True),
        lax.all_to_all(send_bins, ("panels", "cols"), split_axis=1, concat_axis=1, tiled=True),
    )
    matches = (recv_bins[0][:, None] == jnp.arange(STATIONS, dtype=jnp.int32)[None, :]).astype(
        jnp.float32
    )
    station_loads = jnp.dot(recv_values, matches, precision=HIGH)
    station_place = (owner_index * STATIONS + jnp.arange(STATIONS, dtype=jnp.int32)).astype(
        jnp.float32
    ) / (STATIONS * owners)
    placed_loads = station_loads * station_place[None, :]
    own_total = jnp.sum(station_loads, axis=1)
    own_arm = jnp.sum(placed_loads, axis=1)
    zero_row = jnp.zeros_like(own_total)
    prior_total, prior_arm = prefix(
        (own_total, own_arm), ("panels", "cols"), add_pairs, (zero_row, zero_row)
    )
    station_rank = jnp.arange(STATIONS, dtype=jnp.int32)
    inclusive = (station_rank[:, None] <= station_rank[None, :]).astype(jnp.float32)
    strict = (station_rank[:, None] < station_rank[None, :]).astype(jnp.float32)
    running = prior_total[:, None] + jnp.dot(station_loads, inclusive, precision=HIGH)
    earlier = prior_total[:, None] + jnp.dot(station_loads, strict, precision=HIGH)
    moment_arm = prior_arm[:, None] + jnp.dot(placed_loads, strict, precision=HIGH)
    inv_root = 1.0 / math.sqrt(panels_total)
    shear = (running * inv_root).reshape(variant_dev, load_count, STATIONS)
    moment = ((station_place[None, :] * earlier - moment_arm) * inv_root).reshape(
        variant_dev, load_count, STATIONS
    )
    return (shear, moment)


def solution(mesh):
    return jax.shard_map(
        shards,
        mesh=mesh,
        in_specs=(
            P(None, ("groups", "panels", "cols")),
            P(),
            P("groups", None, None),
            P(None, ("groups", "panels", "cols")),
            P(("groups", "panels", "cols")),
            P(("groups", "panels", "cols"), None),
            P("groups"),
            P(),
        ),
        out_specs=(
            P(("groups", "phase"), None, ("panels", "cols")),
            P(("groups", "phase"), None, ("panels", "cols")),
        ),
        check_vma=False,
    )
```

profile of v0, /device:TPU:0, one launch (start us, length us, event | category | flops | bytes accessed | tf_op | source)
XLA Modules:
  0.0 130.9 jit_solution(7332633443924360634)
XLA Ops:
  7.2 0.9 fusion.63
  8.2 0.6 copy-done.4
  8.8 0.6 dynamic_slice.17
  9.4 0.9 fusion.48
  10.3 0.4 convolution_add_fusion.3
  10.8 0.7 copy-done.1
  11.5 0.6 gather_fusion.2
  12.1 0.6 gather_fusion
  12.7 0.6 gather_fusion.1
  13.4 0.2 fusion.60
  14.0 0.1 copy.52
  14.1 5.5 %all_gather.26 = f32[1,3,128]{1,2,0:T(8,128)S(1)} all-gather(f32[1,3,64]{1,2,0:T(8,128)S(1)} %get-tuple-element.175), channel_id=1, replica_groups=mesh['groups'=2,'panels'=4,'cols'=2,'phase'=2] {'cols'}, dimensions={2}, use_global_device_ids=true | all-gather | bytes 2304 | tf_op jit(solution)/shard_map/all_gather | solution.py:124
  19.6 14.1 %all_gather.25 = f32[1,4,256]{1,0,2:T(1,128)S(1)} all-gather(f32[1,4,64]{1,0,2:T(1,128)S(1)} %bitcast.124), channel_id=1, replica_groups=mesh['groups'=2,'panels'=4,'cols'=2,'phase'=2] {'panels'}, dimensions={2}, use_global_device_ids=true | all-gather | bytes 5120 | tf_op jit(solution)/shard_map/all_gather | solution.py:123
  33.8 3.3 %fusion.25 = (f32[256]{0:T(256)S(1)}, f32[256]{0:T(256)S(1)}, f32[256]{0:T(256)S(1)}, f32[256]{0:T(256)S(1)}) fusion(f32[1,4,256]{1,0,2:T(1,128)S(1)} %all_gather.25), kind=kLoop, calls=%fused_computation.44 | loop fusion | flops 256 | bytes 8192 | tf_op jit(solution)/shard_map/mul | solution.py:51
  37.1 0.7 copy-done.3
  37.8 0.2 fusion.64
  38.1 13.2 %all_gather.24 = bf16[1,64,256]{1,2,0:T(8,128)(2,1)S(1)} all-gather(bf16[1,64,64]{1,2,0:T(8,128)(2,1)S(1)} %get-tuple-element.192), channel_id=1, replica_groups=mesh['groups'=2,'panels'=4,'cols'=2,'phase'=2] {'panels'}, dimensions={2}, use_global_device_ids=true | all-gather | bytes 40960 | tf_op jit(solution)/shard_map/all_gather | solution.py:132
  51.3 0.2 slice_reduce_fusion.5
  51.5 0.9 convolution_bitcast_fusion.1
  52.4 0.6 copy-done.5
  53.1 0.2 convert_reduce_fusion
  53.3 0.1 select_reduce_fusion
  53.4 0.7 all_to_all.14
  54.1 5.7 %all-to-all-start.1 = ((s32[1,8,20]{2,0,1:T(1,128)}), s32[1,8,20]{2,0,1:T(1,128)S(1)}, u32[]{:S(2)}, u32[]{:S(2)}) async-start(s32[1,8,20]{2,0,1:T(1,128)} %all_to_all.14), calls=%async_computation.2 | async-start | bytes 8192 | tf_op jit(solution)/shard_map/all_to_all | solution.py:159
  59.8 0.6 copy-done.7
  60.5 0.7 dynamic-slice
  61.8 1.9 %reduce-scatter.5.cloned.1.call-done = f32[1,64,64]{1,2,0:T(8,128)} async-done(((f32[1,64,128]{1,2,0:T(8,128)}), f32[1,64,64]{1,2,0:T(8,128)}) %reduce-scatter.5.cloned.1.call-update) | async-done | bytes 16400 | tf_op jit(solution)/shard_map/reduce_scatter | solution.py:135
  63.7 0.8 add_convert_fusion
  64.4 13.2 %all_gather.27 = bf16[1,64,256]{1,2,0:T(8,128)(2,1)S(1)} all-gather(bf16[1,64,64]{1,2,0:T(8,128)(2,1)S(1)} %add_convert_fusion), channel_id=1, replica_groups=mesh['groups'=2,'panels'=4,'cols'=2,'phase'=2] {'panels'}, dimensions={2}, use_global_device_ids=true | all-gather | bytes 40960 | tf_op jit(solution)/shard_map/all_gather | solution.py:132
  77.7 0.9 convolution_bitcast_fusion
  78.6 10.1 %reduce-scatter.7.cloned.1.call-done = f32[64,64]{1,0:T(8,128)} async-done(((f32[128,64]{1,0:T(8,128)}), f32[64,64]{1,0:T(8,128)}) %reduce-scatter.7.cloned.1.call-update) | async-done | bytes 16400
  88.6 0.8 copy.58
  89.5 0.3 fusion.65
  89.7 0.7 reshape.458
  90.4 4.6 %all-to-all-start = ((f32[8,1,1280]{2,1,0:T(1,128)}), f32[8,1,1280]{2,1,0:T(1,128)S(1)}, u32[]{:S(2)}, u32[]{:S(2)}) async-start(f32[8,1,1280]{2,1,0:T(1,128)} %reshape.458), calls=%async_computation.1 | async-start | bytes 81920 | tf_op jit(solution)/shard_map/all_to_all | solution.py:158
  95.1 0.5 broadcast.246
  95.6 0.7 reduce.21
  96.3 5.5 %all-to-all-done = f32[8,1,1280]{2,1,0:T(1,128)S(1)} async-done(((f32[8,1,1280]{2,1,0:T(1,128)}), f32[8,1,1280]{2,1,0:T(1,128)S(1)}, u32[]{:S(2)}, u32[]{:S(2)}) %all-to-all-start) | async-done | bytes 40992 | tf_op jit(solution)/shard_map/all_to_all | solution.py:158
  101.8 0.5 broadcast.247
  102.3 0.7 reduce.25
  103.2 0.4 multiply_reduce_fusion
  103.6 0.2 dynamic-update-slice
  103.8 0.2 dynamic-update-slice.1
  104.0 17.8 %all-reduce.2 = (f32[512]{0:T(512)S(1)}, f32[512]{0:T(512)S(1)}) all-reduce(f32[512]{0:T(512)S(1)} %dynamic-update-slice, f32[512]{0:T(512)S(1)} %dynamic-update-slice.1), channel_id=2, replica_groups=mesh['groups'=2,'panels'=4,'cols'=2,'phase'=2] {'panels','cols'}, use_global_device_ids=true, to_apply=%add | all-reduce | flops 1024 | bytes 8192
  122.0 0.3 while.16
  122.3 0.2 fusion.3
  122.5 0.8 fusion.5
  123.3 0.8 fusion.2
  (52 shorter events, 1.2 us)
Async XLA Ops:
  7.2 2.2 %copy-start = (f32[2,3,2048]{2,0,1:T(2,128)S(1)}, f32[2,3,2048]{2,0,1:T(2,128)}, u32[]{:S(2)}) copy-start(f32[2,3,2048]{2,0,1:T(2,128)} %param.14) | copy-start | bytes 147460
  7.2 56.5 %reduce-scatter.5.cloned.1.call-start = ((), (), s32[]{:S(2)}) async-start(), calls=%async_computation.4 | async-start | bytes 98304 | tf_op jit(solution)/shard_map/reduce_scatter | solution.py:135
  7.2 0.9 copy-start.2
  8.2 0.7 copy-start.4
  10.8 0.7 copy-start.1
  33.8 3.3 %copy-start.6 = (s32[64]{0:T(128)S(1)}, s32[64]{0:T(128)}, u32[]{:S(2)}) copy-start(s32[64]{0:T(128)} %param.16) | copy-start | bytes 772
  37.1 0.7 copy-start.3
  52.4 0.7 copy-start.5
  54.1 36.4 %all-to-all-start.1 = ((s32[1,8,20]{2,0,1:T(1,128)}), s32[1,8,20]{2,0,1:T(1,128)S(1)}, u32[]{:S(2)}, u32[]{:S(2)}) async-start(s32[1,8,20]{2,0,1:T(1,128)} %all_to_all.14), calls=%async_computation.2 | async-start | bytes 8192 | tf_op jit(solution)/shard_map/all_to_all | solution.py:159
  59.7 28.9 %reduce-scatter.7.cloned.1.call-start = ((), (), s32[]{:S(2)}) async-start(), calls=%async_computation.5 | async-start | bytes 98304
  59.8 0.7 copy-start.7
  90.4 11.4 %all-to-all-start = ((f32[8,1,1280]{2,1,0:T(1,128)}), f32[8,1,1280]{2,1,0:T(1,128)S(1)}, u32[]{:S(2)}, u32[]{:S(2)}) async-start(f32[8,1,1280]{2,1,0:T(1,128)} %reshape.458), calls=%async_computation.1 | async-start | bytes 81920 | tf_op jit(solution)/shard_map/all_to_all | solution.py:158
Sparse Core Ops, SparseCore 0:
  52.5 11.1 reduce-scatter.4
  78.7 9.9 reduce-scatter.6
where the time goes:
time: 131 us
  blocking collectives  63.9 us (49%)
  waiting for transfers between devices  17.4 us (13%)
  between operations  15 us (11%)
  local copies, waits for them, and re-layouts  11.9 us (9%)
  starting transfers between devices  10.4 us (8%)
  other arithmetic  6.43 us (5%)
  matrix products  5.69 us (4%)
    all_gather x2, blocking collectives, apply_influence(): lax.all_gather(strengths, 'panels', axis=2, tiled=True)  26.4 us
    unnamed x1, blocking collectives  17.8 us
    all_gather x1, blocking collectives, shards(): sources = lax.all_gather(own_geometry, 'panels', axis=2, tiled=True)  14.1 us
    unnamed x3, waiting for transfers between devices  10.1 us
    unnamed x24, local copies, waits for them, and re-layouts  6.08 us
    all_to_all x1, starting transfers between devices, shards(): lax.all_to_all(send_bins, ('panels', 'cols'), split_axis=1, concat_axis=1...  5.67 us
    all_gather x1, blocking collectives, shards(): row_targets = lax.all_gather(centroid, 'cols', axis=2, tiled=True)  5.51 us
    all_to_all x1, waiting for transfers between devices, shards(): lax.all_to_all(send_values, ('panels', 'cols'), split_axis=1, concat_axis...  5.47 us
  transfers between devices with their start and end apart: 4, of which 3 were waited for; matrix products, arithmetic and copies ran while one was open for 4% of the time, Pallas kernels for 0%

commit v1 on v0

--- a/solution.py
+++ b/solution.py
@@ -8,6 +8,18 @@
 HIGH = lax.Precision.HIGHEST
 CORE_SQUARE = 0.0025
 SKIN_SQUARE = 0.01
+
+
+def doubled_up(shard, axis, dim):
+    ways, here, hop = (lax.axis_size(axis), lax.axis_index(axis), shard.shape[dim])
+    line, have = (shard, 1)
+    while have < ways:
+        line = jnp.concatenate(
+            [line, lax.ppermute(line, axis, [(d, (d - have) % ways) for d in range(ways)])],
+            axis=dim,
+        )
+        have = 2 * have
+    return jnp.roll(line, here * hop, axis=dim)
 
 
 def prefix(shard, axis, combine, identity):
@@ -126,11 +138,7 @@
     def apply_influence(strengths):
         empty_sum = jnp.zeros((variant_dev, load_count, row_targets.shape[2]), jnp.float32)
         partial_sums = tile_product(
-            empty_sum,
-            row_targets,
-            sources,
-            lax.all_gather(strengths, "panels", axis=2, tiled=True),
-            kernel_scale,
+            empty_sum, row_targets, sources, doubled_up(strengths, "panels", 2), kernel_scale
         )
         return lax.psum_scatter(partial_sums, "cols", scatter_dimension=2, tiled=True)
 

time: 131 us -> 125 us (0.954)
  blocking collectives: 63.9 us -> 35.9 us
  waiting for transfers between devices: 17.4 us -> 29.2 us
  starting transfers between devices: 10.4 us -> 19.9 us
    all_gather x2 -> x0, blocking collectives: 26.4 us -> none  [apply_influence(): lax.all_gather(strengths, 'panels', axis=2, tiled=True)]
    ppermute x0 -> x4, starting transfers between devices: none -> 11.9 us  [doubled_up(): lax.ppermute(line, axis, [(d, (d - have) % ways) for d in range(ways)])]
    unnamed x3 -> x4, waiting for transfers between devices: 10.1 us -> 19.9 us
    ppermute x0 -> x4, waiting for transfers between devices: none -> 3.83 us  [doubled_up(): lax.ppermute(line, axis, [(d, (d - have) % ways) for d in range(ways)])]
    all_to_all x1, starting transfers between devices: 5.67 us -> 3.31 us  [shards(): lax.all_to_all(send_bins, ('panels', 'cols'), split_axis=1, concat_axis=1...]
    reduce_scatter x1 -> x0, waiting for transfers between devices: 1.86 us -> none  [apply_influence(): lax.psum_scatter(partial_sums, 'cols', scatter_dimension=2, tiled=True)]
    unnamed x24 -> x25, local copies, waits for them, and re-layouts: 6.08 us -> 7 us
  transfers between devices with their start and end apart: 4 -> 8, of which waited for: 3 -> 4; matrix products, arithmetic and copies ran while one was open for 4% -> 7% of each run, Pallas kernels for 0% -> 0%
where the time goes in v1:
time: 125 us
  blocking collectives  35.9 us (29%)
  waiting for transfers between devices  29.2 us (23%)
  starting transfers between devices  19.9 us (16%)
  between operations  15 us (12%)
  local copies, waits for them, and re-layouts  12.8 us (10%)
  matrix products  5.87 us (5%)
  other arithmetic  5.84 us (5%)
    unnamed x4, waiting for transfers between devices  19.9 us
    unnamed x1, blocking collectives  17.8 us
    all_gather x1, blocking collectives, shards(): sources = lax.all_gather(own_geometry, 'panels', axis=2, tiled=True)  13.5 us
    ppermute x4, starting transfers between devices, doubled_up(): lax.ppermute(line, axis, [(d, (d - have) % ways) for d in range(ways)])  11.9 us
    unnamed x25, local copies, waits for them, and re-layouts  7 us
    all_to_all x1, waiting for transfers between devices, shards(): lax.all_to_all(send_values, ('panels', 'cols'), split_axis=1, concat_axis...  5.47 us
    all_to_all x1, starting transfers between devices, shards(): lax.all_to_all(send_values, ('panels', 'cols'), split_axis=1, concat_axis...  4.61 us
    all_gather x1, blocking collectives, shards(): row_targets = lax.all_gather(centroid, 'cols', axis=2, tiled=True)  4.58 us
  transfers between devices with their start and end apart: 8, of which 4 were waited for; matrix products, arithmetic and copies ran while one was open for 7% of the time, Pallas kernels for 0%

profile of v1, /device:TPU:0, one launch (start us, length us, event | category | flops | bytes accessed | tf_op | source)
XLA Modules:
  0.0 124.7 jit_solution(1848303088340533278)
XLA Ops:
  7.2 0.7 copy-done.2
  7.9 0.9 fusion.81
  8.8 0.6 copy-done.4
  9.5 0.6 dynamic_slice.20
  10.1 0.9 fusion.64
  10.9 0.4 convolution_add_fusion.3
  11.5 0.7 copy-done.1
  12.2 0.6 gather_fusion
  12.8 0.6 gather_fusion.2
  13.4 0.6 gather_fusion.1
  14.2 0.2 fusion.78
  14.4 0.7 copy-done.3
  15.1 0.2 fusion.82
  15.3 5.1 %collective-permute-start = (bf16[1,64,64]{2,1,0:T(8,128)(2,1)S(1)}, bf16[1,64,64]{2,1,0:T(8,128)(2,1)S(1)}, u32[]{:S(2)}, u32[]{:S(2)}) collective-permute-start(bf16[1,64,64]{2,1,0:T(8,128)(2,1)S(1)} %get-tuple-element.193), channel_id=1, source_target_pairs={{0,12},{4,0},{8,4},{12,8},{1,13},{5,1},{9,5},{13,9},{2,14},{6,2},{... | collective-permute-start | bytes 24584 | tf_op jit(solution)/shard_map/ppermute | solution.py:18
  20.5 0.2 convert_reduce_fusion
  21.1 13.5 %all_gather.18 = f32[1,4,256]{1,0,2:T(1,128)S(1)} all-gather(f32[1,4,64]{1,0,2:T(1,128)S(1)} %bitcast.132), channel_id=1, replica_groups=mesh['groups'=2,'panels'=4,'cols'=2,'phase'=2] {'panels'}, dimensions={2}, use_global_device_ids=true | all-gather | bytes 5120 | tf_op jit(solution)/shard_map/all_gather | solution.py:135
  34.6 3.3 %fusion.25 = (f32[256]{0:T(256)S(1)}, f32[256]{0:T(256)S(1)}, f32[256]{0:T(256)S(1)}, f32[256]{0:T(256)S(1)}) fusion(f32[1,4,256]{1,0,2:T(1,128)S(1)} %all_gather.18), kind=kLoop, calls=%fused_computation.44 | loop fusion | flops 256 | bytes 8192 | tf_op jit(solution)/shard_map/mul | solution.py:63
  37.9 4.6 %all_gather.19 = f32[1,3,128]{1,2,0:T(8,128)S(1)} all-gather(f32[1,3,64]{1,2,0:T(8,128)S(1)} %get-tuple-element.176), channel_id=1, replica_groups=mesh['groups'=2,'panels'=4,'cols'=2,'phase'=2] {'cols'}, dimensions={2}, use_global_device_ids=true | all-gather | bytes 2304 | tf_op jit(solution)/shard_map/all_gather | solution.py:136
  42.6 0.6 collective-permute-start.1
  43.2 0.2 slice_reduce_fusion.5
  43.4 3.8 %collective-permute-done.1 = bf16[1,64,128]{2,1,0:T(8,128)(2,1)S(1)} collective-permute-done((bf16[1,64,128]{2,1,0:T(8,128)(2,1)S(1)}, bf16[1,64,128]{2,1,0:T(8,128)(2,1)S(1)}, u32[]{:S(2)}, u32[]{:S(2)}) %collective-permute-start.1) | collective-permute-done | bytes 16416 | tf_op jit(solution)/shard_map/ppermute | solution.py:18
  47.2 1.0 convolution_bitcast_fusion.1
  48.3 8.4 %reduce-scatter.7.cloned.1.call-done = f32[64,64]{1,0:T(8,128)} async-done(((f32[128,64]{1,0:T(8,128)}), f32[64,64]{1,0:T(8,128)}) %reduce-scatter.7.cloned.1.call-update) | async-done | bytes 16400
  56.7 0.8 copy.51
  57.5 3.4 %collective-permute-start.2 = (bf16[1,64,64]{2,1,0:T(8,128)(2,1)S(1)}, bf16[1,64,64]{2,1,0:T(8,128)(2,1)S(1)}, u32[]{:S(2)}, u32[]{:S(2)}) collective-permute-start(bf16[1,64,64]{2,1,0:T(8,128)(2,1)S(1)} %add_convert_fusion), channel_id=1, source_target_pairs={{0,12},{4,0},{8,4},{12,8},{1,13},{5,1},{9,5},{13,9},{2,14},{6,2},{... | collective-permute-start | bytes 24584 | tf_op jit(solution)/shard_map/ppermute | solution.py:18
  61.0 0.7 all_to_all.14
  61.7 3.3 %all-to-all-start.1 = ((s32[1,8,20]{2,0,1:T(1,128)}), s32[1,8,20]{2,0,1:T(1,128)S(1)}, u32[]{:S(2)}, u32[]{:S(2)}) async-start(s32[1,8,20]{2,0,1:T(1,128)} %all_to_all.14), calls=%async_computation.1 | async-start | bytes 8192 | tf_op jit(solution)/shard_map/all_to_all | solution.py:167
  65.2 2.8 %collective-permute-start.3 = (bf16[1,64,128]{2,1,0:T(8,128)(2,1)S(1)}, bf16[1,64,128]{2,1,0:T(8,128)(2,1)S(1)}, u32[]{:S(2)}, u32[]{:S(2)}) collective-permute-start(bf16[1,64,128]{2,1,0:T(8,128)(2,1)S(1)} %pad_maximum_fusion.2), channel_id=1, source_target_pairs={{0,8},{4,12},{8,0},{12,4},{1,9},{5,13},{9,1},{13,5},{2,10},{6,14},... | collective-permute-start | bytes 49160 | tf_op jit(solution)/shard_map/ppermute | solution.py:18
  68.0 0.7 copy-done.7
  68.6 0.7 dynamic-slice
  70.0 1.0 convolution_bitcast_fusion
  71.0 11.4 %reduce-scatter.9.cloned.1.call-done = f32[64,64]{1,0:T(8,128)} async-done(((f32[128,64]{1,0:T(8,128)}), f32[64,64]{1,0:T(8,128)}) %reduce-scatter.9.cloned.1.call-update) | async-done | bytes 16400
  82.4 0.8 copy.53
  83.3 0.3 fusion.83
  83.5 0.7 reshape.460
  84.2 4.6 %all-to-all-start = ((f32[8,1,1280]{2,1,0:T(1,128)}), f32[8,1,1280]{2,1,0:T(1,128)S(1)}, u32[]{:S(2)}, u32[]{:S(2)}) async-start(f32[8,1,1280]{2,1,0:T(1,128)} %reshape.460), calls=%async_computation | async-start | bytes 81920 | tf_op jit(solution)/shard_map/all_to_all | solution.py:166
  88.9 0.5 broadcast.247
  89.4 0.7 reduce.21
  90.1 5.5 %all-to-all-done = f32[8,1,1280]{2,1,0:T(1,128)S(1)} async-done(((f32[8,1,1280]{2,1,0:T(1,128)}), f32[8,1,1280]{2,1,0:T(1,128)S(1)}, u32[]{:S(2)}, u32[]{:S(2)}) %all-to-all-start) | async-done | bytes 40992 | tf_op jit(solution)/shard_map/all_to_all | solution.py:166
  95.6 0.5 broadcast.248
  96.1 0.7 reduce.25
  96.9 0.4 multiply_reduce_fusion
  97.3 0.2 dynamic-update-slice
  97.6 0.2 dynamic-update-slice.1
  97.8 17.8 %all-reduce.2 = (f32[512]{0:T(512)S(1)}, f32[512]{0:T(512)S(1)}) all-reduce(f32[512]{0:T(512)S(1)} %dynamic-update-slice, f32[512]{0:T(512)S(1)} %dynamic-update-slice.1), channel_id=2, replica_groups=mesh['groups'=2,'panels'=4,'cols'=2,'phase'=2] {'panels','cols'}, use_global_device_ids=true, to_apply=%add | all-reduce | flops 1024 | bytes 8192
  115.8 0.3 while.16
  116.1 0.8 fusion.5
  117.0 0.8 fusion.2
  (61 shorter events, 1.8 us)
Async XLA Ops:
  7.2 2.9 %copy-start = (f32[2,3,2048]{2,0,1:T(2,128)S(1)}, f32[2,3,2048]{2,0,1:T(2,128)}, u32[]{:S(2)}) copy-start(f32[2,3,2048]{2,0,1:T(2,128)} %param.16) | copy-start | bytes 147460
  7.2 49.5 %reduce-scatter.7.cloned.1.call-start = ((), (), s32[]{:S(2)}) async-start(), calls=%async_computation.4 | async-start | bytes 98304
  7.2 0.7 copy-start.2
  8.8 0.7 copy-start.4
  11.5 0.7 copy-start.1
  13.4 0.7 copy-start.6
  14.4 0.7 copy-start.3
  15.3 5.1 %copy-start.5 = (s32[64,1]{0,1:T(1,128)S(1)}, s32[64,1]{0,1:T(1,128)}, u32[]{:S(2)}) copy-start(s32[64,1]{0,1:T(1,128)} %param.19) | copy-start | bytes 772
  15.3 27.2 %collective-permute-start = (bf16[1,64,64]{2,1,0:T(8,128)(2,1)S(1)}, bf16[1,64,64]{2,1,0:T(8,128)(2,1)S(1)}, u32[]{:S(2)}, u32[]{:S(2)}) collective-permute-start(bf16[1,64,64]{2,1,0:T(8,128)(2,1)S(1)} %get-tuple-element.193), channel_id=1, source_target_pairs={{0,12},{4,0},{8,4},{12,8},{1,13},{5,1},{9,5},{13,9},{2,14},{6,2},{... | collective-permute-start | bytes 24584 | tf_op jit(solution)/shard_map/ppermute | solution.py:18
  42.6 4.6 %collective-permute-start.1 = (bf16[1,64,128]{2,1,0:T(8,128)(2,1)S(1)}, bf16[1,64,128]{2,1,0:T(8,128)(2,1)S(1)}, u32[]{:S(2)}, u32[]{:S(2)}) collective-permute-start(bf16[1,64,128]{2,1,0:T(8,128)(2,1)S(1)} %pad_maximum_fusion.1), channel_id=1, source_target_pairs={{0,8},{4,12},{8,0},{12,4},{1,9},{5,13},{9,1},{13,5},{2,10},{6,14},... | collective-permute-start | bytes 49160 | tf_op jit(solution)/shard_map/ppermute | solution.py:18
  57.5 7.5 %collective-permute-start.2 = (bf16[1,64,64]{2,1,0:T(8,128)(2,1)S(1)}, bf16[1,64,64]{2,1,0:T(8,128)(2,1)S(1)}, u32[]{:S(2)}, u32[]{:S(2)}) collective-permute-start(bf16[1,64,64]{2,1,0:T(8,128)(2,1)S(1)} %add_convert_fusion), channel_id=1, source_target_pairs={{0,12},{4,0},{8,4},{12,8},{1,13},{5,1},{9,5},{13,9},{2,14},{6,2},{... | collective-permute-start | bytes 24584 | tf_op jit(solution)/shard_map/ppermute | solution.py:18
  61.7 22.5 %all-to-all-start.1 = ((s32[1,8,20]{2,0,1:T(1,128)}), s32[1,8,20]{2,0,1:T(1,128)S(1)}, u32[]{:S(2)}, u32[]{:S(2)}) async-start(s32[1,8,20]{2,0,1:T(1,128)} %all_to_all.14), calls=%async_computation.1 | async-start | bytes 8192 | tf_op jit(solution)/shard_map/all_to_all | solution.py:167
  65.0 17.4 %reduce-scatter.9.cloned.1.call-start = ((), (), s32[]{:S(2)}) async-start(), calls=%async_computation.5 | async-start | bytes 98304
  65.2 4.8 %collective-permute-start.3 = (bf16[1,64,128]{2,1,0:T(8,128)(2,1)S(1)}, bf16[1,64,128]{2,1,0:T(8,128)(2,1)S(1)}, u32[]{:S(2)}, u32[]{:S(2)}) collective-permute-start(bf16[1,64,128]{2,1,0:T(8,128)(2,1)S(1)} %pad_maximum_fusion.2), channel_id=1, source_target_pairs={{0,8},{4,12},{8,0},{12,4},{1,9},{5,13},{9,1},{13,5},{2,10},{6,14},... | collective-permute-start | bytes 49160 | tf_op jit(solution)/shard_map/ppermute | solution.py:18
  68.0 0.7 copy-start.7
  84.2 11.3 %all-to-all-start = ((f32[8,1,1280]{2,1,0:T(1,128)}), f32[8,1,1280]{2,1,0:T(1,128)S(1)}, u32[]{:S(2)}, u32[]{:S(2)}) async-start(f32[8,1,1280]{2,1,0:T(1,128)} %reshape.460), calls=%async_computation | async-start | bytes 81920 | tf_op jit(solution)/shard_map/all_to_all | solution.py:166
Sparse Core Ops, SparseCore 0:
  48.4 8.2 reduce-scatter.6
  71.1 11.2 reduce-scatter.8
